TPU v7x, 32 devices: a whole 2x2x4 slice. The times are simulated.
32 devices in a mesh: stn: 8 (over z, x), chan: 4 (over y, core).
Axes of the slice: x: 2, y: 2, z: 4, core: 2. Of those that a mesh axis runs over, the one named last changes fastest.
Arguments:
- samples: bfloat16 [64, 17, 2, 8192], P(('stn', 'chan')), may hold values from -6 to 6
- keeper: int32 [8, 8], replicated, may hold values from 0 to 1, as said below
Outputs:
- visibilities: bfloat16 [64, 2, 4096, 40], P('stn', None, 'chan')
Inputs may be any that keep to these rules, and one draw needn't show every extreme that they name: keeper[g, g] is 1; for g != h with d = (g - h) mod 8: keeper[g, h] is 1 where 0 < d < 4, 0 where d > 4, and at d = 4 exactly one of keeper[g, h] and keeper[h, g] is 1, which one drawn for each such pair; half of the rows hold 5 ones, the others 5 - 1.
All inputs are finite; a program needn't handle non-finite values.
Results may differ from a plain program's by a relative error of at most 0.0077.
Values may be sent and summed in bfloat16 or wider, within the bound.
A program may use at most 192 MiB of HBM per device.

v0:
```python
import math
import jax
import jax.numpy as jnp
from jax import lax
from jax.sharding import PartitionSpec as P

NFFT = 8192
TAPS = 16
CH_WIN = 1024
DFT_BLOCK = 256


def from_behind(value, axis, by):
    devices = lax.axis_size(axis)
    return lax.ppermute(value, axis, [(i, (i + by) % devices) for i in range(devices)])


def taps_table():
    pos = jnp.arange(TAPS * NFFT).astype(jnp.float32)
    shifted = (pos + 0.5) / NFFT - TAPS / 2.0
    window = 0.5 - 0.5 * jnp.cos(2.0 * math.pi * (pos + 0.5) / (TAPS * NFFT))
    return (jnp.sinc(shifted) * window).reshape(TAPS, NFFT)


def twiddles(width):
    index_n = jnp.arange(NFFT, dtype=jnp.int32)[:, None]
    index_k = jnp.arange(width, dtype=jnp.int32)[None, :]
    phase = (index_n * index_k % NFFT).astype(jnp.float32) * (2.0 * math.pi / NFFT)
    cosines = jnp.cos(phase).astype(jnp.bfloat16)
    sines = jnp.sin(phase).astype(jnp.bfloat16)
    upper = jnp.concatenate([cosines, -sines], axis=1)
    lower = jnp.concatenate([sines, cosines], axis=1)
    return jnp.concatenate([upper, lower], axis=0)


def rotations(ch_tot, width):
    blocks = ch_tot // width
    index_n = jnp.arange(NFFT, dtype=jnp.int32)[None, :]
    index_b = jnp.arange(blocks, dtype=jnp.int32)[:, None]
    phase = (index_n * index_b * width % NFFT).astype(jnp.float32) * (2.0 * math.pi / NFFT)
    return (jnp.cos(phase), jnp.sin(phase))


def channelise(block, taps, table, cos_rot, sin_rot, ch_tot):
    frames = block.shape[1] - TAPS + 1
    count = block.shape[0]
    width = table.shape[1] // 2
    blocks = ch_tot // width
    total = taps[0] * block[:, 0:frames].astype(jnp.float32)
    for tap in range(1, TAPS):
        total = total + taps[tap] * block[:, tap : tap + frames].astype(jnp.float32)
    real_part = total[:, :, 0][None]
    imag_part = total[:, :, 1][None]
    cosine = cos_rot[:, None, None, :]
    sine = sin_rot[:, None, None, :]
    rot_real = real_part * cosine + imag_part * sine
    rot_imag = imag_part * cosine - real_part * sine
    lhs = jnp.stack([rot_real, rot_imag], axis=3).astype(jnp.bfloat16)
    lhs = lhs.reshape(blocks * count * frames, 2 * NFFT)
    spectrum = jnp.dot(lhs, table, preferred_element_type=jnp.float32) * (1.0 / math.sqrt(NFFT))
    spectrum = spectrum.astype(jnp.bfloat16).reshape(blocks, count, frames, 2, width)
    spectrum = jnp.transpose(spectrum, (1, 0, 4, 3, 2))
    return spectrum.reshape(count, ch_tot, 2, frames)


def correlate(own, others, frames):
    half = others.shape[2] // 2
    turned = jnp.concatenate([-others[:, :, half:], others[:, :, :half]], axis=2)
    rhs = jnp.concatenate([others, turned], axis=0)
    product = lax.dot_general(
        own, rhs, (((2,), (2,)), ((1,), (1,))), preferred_element_type=jnp.float32
    )
    rows = others.shape[0]
    product = product.reshape(product.shape[0], product.shape[1], 2, rows)
    return jnp.transpose(product, (1, 2, 0, 3)) / frames


def slot_table(keep_rows, keep_slots):
    ranking = jnp.cumsum(keep_rows, axis=1) - 1
    slot_index = jnp.arange(keep_slots, dtype=jnp.int32)
    matched = (keep_rows[:, :, None] == 1) & (ranking[:, :, None] == slot_index[None, None, :])
    column_ids = jnp.arange(keep_rows.shape[1], dtype=jnp.int32)
    slot_column = jnp.sum(jnp.where(matched, column_ids[None, :, None], 0), axis=1)
    filled = jnp.any(matched, axis=1)
    return (slot_column, filled)


def per_device(samples, keeper):
    n_chan = lax.axis_size("chan")
    n_stn = lax.axis_size("stn")
    ch_tot = CH_WIN * n_chan
    frames = samples.shape[1] - TAPS + 1
    cos_rot, sin_rot = rotations(ch_tot, DFT_BLOCK)
    spectrum = channelise(samples, taps_table(), twiddles(DFT_BLOCK), cos_rot, sin_rot, ch_tot)
    local = lax.all_to_all(spectrum, "chan", split_axis=1, concat_axis=0, tiled=True)
    group_in = local.shape[0]
    own = local.reshape(group_in, CH_WIN, 2 * frames)
    keep_slots = n_stn // 2 + 1
    group_index = lax.axis_index("stn")
    row_keep = jnp.take(keeper, group_index, axis=0)
    slot_column, filled = slot_table(row_keep[None], keep_slots)
    slot_column = slot_column[0]
    filled = filled[0]
    nothing = jnp.zeros((), jnp.bfloat16)
    half = n_stn // 2
    stacked = own[None]
    stride = 1
    while stride < half:
        moved = from_behind(stacked, "stn", stride)
        stacked = jnp.concatenate([stacked, moved], axis=0)
        stride = stride * 2
    far_group = from_behind(own, "stn", half)
    partners = jnp.concatenate([stacked, far_group[None]], axis=0)
    partners = partners.reshape((half + 1) * group_in, CH_WIN, 2 * frames)
    tiles = correlate(own, partners, frames).astype(jnp.bfloat16)
    tiles = tiles.reshape(group_in, 2, CH_WIN, half + 1, group_in)
    slot_distance = jnp.minimum((group_index - slot_column) % n_stn, half)
    picked = jnp.take(tiles, slot_distance, axis=3)
    picked = jnp.where(filled[None, None, None, :, None], picked, nothing)
    return picked.reshape(group_in, 2, CH_WIN, keep_slots * group_in)


def solution(mesh):
    placed = (P(("stn", "chan"), None, None, None), P())
    return jax.shard_map(
        per_device,
        mesh=mesh,
        in_specs=placed,
        out_specs=P("stn", None, "chan", None),
        check_vma=False,
    )
```

profile of v0, /device:TPU:0, one launch (start us, length us, event | category | flops | bytes accessed | tf_op | source)
XLA Modules:
  0.0 166.4 jit_solution(14174221383164325046)
XLA Ops:
  0.0 2.4 %fusion.29 = f32[131072]{0:T(1024)S(1)} fusion(), kind=kLoop, calls=%fused_computation.45 | loop fusion | flops 5373952 | bytes 524288 | tf_op jit(solution)/shard_map/mul | solution.py:22
  2.4 2.1 %fusion.41 = (f32[16,8192]{1,0:T(8,128)S(1)}, f32[16,8192]{1,0:T(8,128)S(1)}) fusion(), kind=kLoop, calls=%fused_computation.65 | loop fusion | flops 1966080 | bytes 1048576 | tf_op jit(solution)/shard_map/sin | solution.py:41
  4.5 35.0 %sine_convert_fusion = (bf16[8192,256]{1,0:T(8,128)(2,1)}, bf16[8192,256]{1,0:T(8,128)(2,1)}) fusion(), kind=kLoop, calls=%fused_computation.15 | loop fusion | flops 33554432 | bytes 8388608 | tf_op jit(solution)/shard_map/convert_element_type | solution.py:30
  39.5 32.3 %fusion.14 = bf16[8192,256]{1,0:T(8,128)(2,1)} fusion(), kind=kLoop, calls=%fused_computation.24 | loop fusion | flops 37748736 | bytes 4194304 | tf_op jit(solution)/shard_map/neg | solution.py:31
  71.9 2.1 %multiply_add_fusion.1 = f32[2,2,2,8192]{3,2,1,0:T(2,128)S(1)} fusion(bf16[2,17,2,8192]{3,2,1,0:T(2,128)(2,1)S(1)} %copy-done, f32[8192]{0:T(1024)S(1)} %get-tuple-element.19, f32[8192]{0:T(1024)S(1)} %get-tuple-element.20, f32[8192]{0:T(1024)S(1)} %get-tuple-element.21, f32[8192]{0:T(1024)S(1)} %get-tuple-element.22, f32[8192]{0:T(1024)S(1)} %get-tuple-element.23, ...), kind=kLoop, calls=%fused_computation.67 | loop fusion | flops 3080192 | bytes 2883584 | tf_op jit(solution)/shard_map/add | solution.py:51
  74.0 0.2 fusion.53
  74.2 0.2 copy_bitcast_fusion.1
  74.4 4.4 %add_convert_fusion = (bf16[16,2,2,1,8192]{4,3,2,1,0:T(2,128)(2,1)S(1)}, bf16[16,2,2,1,8192]{4,3,2,1,0:T(2,128)(2,1)S(1)}) fusion(f32[16,8192]{1,0:T(8,128)S(1)} %get-tuple-element.40, f32[2,2,8192]{2,1,0:T(2,128)S(1)} %get-tuple-element.38, f32[16,8192]{1,0:T(8,128)S(1)} %get-tuple-element.41, f32[2,2,8192]{2,1,0:T(2,128)S(1)} %get-tuple-element.39), kind=kLoop, calls=%fused_computation.23 | loop fusion | flops 4194304 | bytes 3407872 | tf_op jit(solution)/shard_map/convert
  78.8 4.8 %pad_maximum_fusion = bf16[16,2,2,2,8192]{4,3,2,1,0:T(2,128)(2,1)S(1)} fusion(bf16[16,2,2,1,8192]{4,3,2,1,0:T(2,128)(2,1)S(1)} %get-tuple-element.17, bf16[16,2,2,1,8192]{4,3,2,1,0:T(2,128)(2,1)S(1)} %get-tuple-element.16), kind=kLoop, calls=%fused_computation.21 | loop fusion | flops 4194304 | bytes 4194304 | tf_op jit(solution)/shard_map/stack | solution.py:58
  83.7 1.2 copy.55
  84.8 13.7 %fusion.19 = bf16[64,512]{1,0:T(8,128)(2,1)S(1)} fusion(bf16[64,16384]{1,0:T(8,128)(2,1)S(1)} %bitcast.50, bf16[8192,256]{1,0:T(8,128)(2,1)} %get-tuple-element.43, bf16[8192,256]{1,0:T(8,128)(2,1)} %get-tuple-element.42, bf16[8192,256]{1,0:T(8,128)(2,1)} %fusion.14), kind=kOutput, calls=%fused_computation.28 | convolution fusion | flops 1140916224 | bytes 14745600 | tf_op jit(solution)/shard_map/dot_general | solution.py:60
  98.6 4.9 %copy.50 = bf16[2,16,256,2,2]{4,3,0,2,1:T(2,128)(2,1)} copy(bf16[2,16,256,2,2]{2,1,4,3,0:T(8,128)(2,1)S(1)} %bitcast.51) | data formatting | bytes 131072 | tf_op jit(solution)/shard_map/reshape | solution.py:63
  103.6 7.8 %reshape.394 = bf16[4,2,4096]{2,1,0:T(2,128)(2,1)} reshape(bf16[4096,2,2,2]{3,2,1,0:T(2,128)(2,1)} %bitcast.46) | data formatting | bytes 131072
  111.3 4.3 %all-to-all-start = ((bf16[4,2,4096]{2,1,0:T(2,128)(2,1)}), bf16[4,2,4096]{2,1,0:T(2,128)(2,1)S(1)}, u32[]{:S(2)}, u32[]{:S(2)}) async-start(bf16[4,2,4096]{2,1,0:T(2,128)(2,1)} %reshape.394), calls=%async_computation | async-start | bytes 131072 | tf_op jit(solution)/shard_map/all_to_all | solution.py:95
  115.6 0.7 fusion.51
  116.3 0.7 compare_bitcast_fusion
  117.2 0.2 select_reduce_fusion
  117.4 2.3 %all-to-all-done = bf16[4,2,4096]{2,1,0:T(2,128)(2,1)S(1)} async-done(((bf16[4,2,4096]{2,1,0:T(2,128)(2,1)}), bf16[4,2,4096]{2,1,0:T(2,128)(2,1)S(1)}, u32[]{:S(2)}, u32[]{:S(2)}) %all-to-all-start) | async-done | bytes 65568 | tf_op jit(solution)/shard_map/all_to_all | solution.py:95
  119.7 10.0 %reshape.395 = bf16[4096,2,2,2]{3,2,1,0:T(2,128)(2,1)} reshape(bf16[4,2,4096]{2,1,0:T(2,128)(2,1)S(1)} %all-to-all-done) | data formatting | bytes 131072
  129.7 9.7 %copy.51 = bf16[2,4,1024,2,2]{2,1,4,3,0:T(4,128)(2,1)S(1)} copy(bf16[2,4,1024,2,2]{4,3,0,2,1:T(2,128)(2,1)} %bitcast.47) | data formatting | bytes 131072 | tf_op jit(solution)/shard_map/all_to_all | solution.py:95
  139.6 2.0 %collective-permute-start = (bf16[1,8,1024,4]{2,1,3,0:T(8,128)(2,1)S(1)}, bf16[1,8,1024,4]{2,1,3,0:T(8,128)(2,1)S(1)}, u32[]{:S(2)}, u32[]{:S(2)}) collective-permute-start(bf16[1,8,1024,4]{2,1,3,0:T(8,128)(2,1)S(1)} %broadcast_in_dim_reshape.3), channel_id=1, source_target_pairs={{0,4},{4,8},{8,12},{12,16},{16,20},{20,24},{24,28},{28,0},{1,5},{5... | collective-permute-start | bytes 196616 | tf_op jit(solution)/shard_map/ppermute | solution.py:15
  141.6 5.3 %collective-permute-done = bf16[1,8,1024,4]{2,1,3,0:T(8,128)(2,1)S(1)} collective-permute-done((bf16[1,8,1024,4]{2,1,3,0:T(8,128)(2,1)S(1)}, bf16[1,8,1024,4]{2,1,3,0:T(8,128)(2,1)S(1)}, u32[]{:S(2)}, u32[]{:S(2)}) %collective-permute-start) | collective-permute-done | bytes 65568 | tf_op jit(solution)/shard_map/ppermute | solution.py:15
  147.0 0.2 fusion.43
  147.5 2.6 %collective-permute-start.2 = (bf16[8,1024,4]{1,0,2:T(8,128)(2,1)S(1)}, bf16[8,1024,4]{1,0,2:T(8,128)(2,1)S(1)}, u32[]{:S(2)}, u32[]{:S(2)}) collective-permute-start(bf16[8,1024,4]{1,0,2:T(8,128)(2,1)S(1)} %reshape.350), channel_id=1, source_target_pairs={{0,16},{4,20},{8,24},{12,28},{16,0},{20,4},{24,8},{28,12},{1,17},{... | collective-permute-start | bytes 196616 | tf_op jit(solution)/shard_map/ppermute | solution.py:15
  150.1 1.4 copy.46
  151.5 4.0 %collective-permute-done.2 = bf16[8,1024,4]{1,0,2:T(8,128)(2,1)S(1)} collective-permute-done((bf16[8,1024,4]{1,0,2:T(8,128)(2,1)S(1)}, bf16[8,1024,4]{1,0,2:T(8,128)(2,1)S(1)}, u32[]{:S(2)}, u32[]{:S(2)}) %collective-permute-start.2) | collective-permute-done | bytes 65568 | tf_op jit(solution)/shard_map/ppermute | solution.py:15
  155.5 1.4 copy.44
  157.0 1.4 copy.45
  158.4 3.8 %multiply_convert_fusion = bf16[1024,8,80]{2,1,0:T(8,128)(2,1)S(1)} fusion(bf16[8,1024,4]{0,2,1:T(4,128)(2,1)} %copy.46, bf16[40,1024,4]{0,2,1:T(4,128)(2,1)} %copy.45, bf16[40,1024,4]{0,2,1:T(4,128)(2,1)} %copy.44), kind=kOutput, calls=%fused_computation.20 | convolution fusion | flops 7864320 | bytes 2031616 | tf_op jit(solution)/shard_map/dot_general | solution.py:70
  162.2 2.0 %copy.47 = bf16[1024,8,80]{0,2,1:T(8,128)(2,1)S(1)} copy(bf16[1024,8,80]{2,1,0:T(8,128)(2,1)S(1)} %multiply_convert_fusion) | data formatting | bytes 2621440 | tf_op jit(solution)/shard_map/convert_element_type | solution.py:115
  164.3 0.6 gather_fusion
  165.0 1.5 fusion.15
  (24 shorter events, 1.1 us)
Async XLA Ops:
  39.5 32.4 %copy-start = (bf16[2,17,2,8192]{3,2,1,0:T(2,128)(2,1)S(1)}, bf16[2,17,2,8192]{3,2,1,0:T(2,128)(2,1)}, u32[]{:S(2)}) copy-start(bf16[2,17,2,8192]{3,2,1,0:T(2,128)(2,1)} %param.2) | copy-start | bytes 3342340
  111.3 8.4 %all-to-all-start = ((bf16[4,2,4096]{2,1,0:T(2,128)(2,1)}), bf16[4,2,4096]{2,1,0:T(2,128)(2,1)S(1)}, u32[]{:S(2)}, u32[]{:S(2)}) async-start(bf16[4,2,4096]{2,1,0:T(2,128)(2,1)} %reshape.394), calls=%async_computation | async-start | bytes 131072 | tf_op jit(solution)/shard_map/all_to_all | solution.py:95
  139.6 7.3 %collective-permute-start = (bf16[1,8,1024,4]{2,1,3,0:T(8,128)(2,1)S(1)}, bf16[1,8,1024,4]{2,1,3,0:T(8,128)(2,1)S(1)}, u32[]{:S(2)}, u32[]{:S(2)}) collective-permute-start(bf16[1,8,1024,4]{2,1,3,0:T(8,128)(2,1)S(1)} %broadcast_in_dim_reshape.3), channel_id=1, source_target_pairs={{0,4},{4,8},{8,12},{12,16},{16,20},{20,24},{24,28},{28,0},{1,5},{5... | collective-permute-start | bytes 196616 | tf_op jit(solution)/shard_map/ppermute | solution.py:15
  146.9 8.6 %collective-permute-start.1 = (bf16[2,8,1024,4]{2,1,3,0:T(8,128)(2,1)S(1)}, bf16[2,8,1024,4]{2,1,3,0:T(8,128)(2,1)S(1)}, u32[]{:S(2)}, u32[]{:S(2)}) collective-permute-start(bf16[2,8,1024,4]{2,1,3,0:T(8,128)(2,1)S(1)} %pad_maximum_fusion.3), channel_id=1, source_target_pairs={{0,8},{4,12},{8,16},{12,20},{16,24},{20,28},{24,0},{28,4},{1,9},{5... | collective-permute-start | bytes 393224 | tf_op jit(solution)/shard_map/ppermute | solution.py:15
  147.5 8.0 %collective-permute-start.2 = (bf16[8,1024,4]{1,0,2:T(8,128)(2,1)S(1)}, bf16[8,1024,4]{1,0,2:T(8,128)(2,1)S(1)}, u32[]{:S(2)}, u32[]{:S(2)}) collective-permute-start(bf16[8,1024,4]{1,0,2:T(8,128)(2,1)S(1)} %reshape.350), channel_id=1, source_target_pairs={{0,16},{4,20},{8,24},{12,28},{16,0},{20,4},{24,8},{28,12},{1,17},{... | collective-permute-start | bytes 196616 | tf_op jit(solution)/shard_map/ppermute | solution.py:15
where the time goes:
time: 167 us; the launch traced here: 166 us
  other arithmetic  86.7 us (52%)
  local copies, waits for them, and re-layouts  41.5 us (25%)
  matrix products  17.5 us (10%)
  waiting for transfers between devices  11.6 us (7%)
  starting transfers between devices  8.94 us (5%)
    convert_element_type x1, other arithmetic, twiddles(): sines = jnp.sin(phase).astype(jnp.bfloat16)  35 us
    neg x1, other arithmetic, twiddles(): upper = jnp.concatenate([cosines, -sines], axis=1)  32.3 us
    unnamed x6, local copies, waits for them, and re-layouts  19.2 us
    dot_general x1, matrix products, channelise(): jnp.dot(lhs, table, preferred_element_type=jnp.float32)  13.7 us
    all_to_all x2, local copies, waits for them, and re-layouts, per_device(): lax.all_to_all(spectrum, 'chan', split_axis=1, concat_axis=0, tiled=True)  9.8 us
    ppermute x3, waiting for transfers between devices, from_behind(): lax.ppermute(value, axis, [(i, (i + by) % devices) for i in range(devices)])  9.25 us
    reshape x1, local copies, waits for them, and re-layouts, channelise(): return spectrum.reshape(count, ch_tot, 2, frames)  4.94 us
    another operation x1, other arithmetic, channelise(): lhs = jnp.stack([rot_real, rot_imag], axis=3).astype(jnp.bfloat16)  4.84 us
  transfers between devices with their start and end apart: 4, of which 3 were waited for; matrix products, arithmetic and copies ran while one was open for 2% of the time, Pallas kernels for 0%

commit v1 on v0

--- a/solution.py
+++ b/solution.py
@@ -92,7 +92,9 @@
     frames = samples.shape[1] - TAPS + 1
     cos_rot, sin_rot = rotations(ch_tot, DFT_BLOCK)
     spectrum = channelise(samples, taps_table(), twiddles(DFT_BLOCK), cos_rot, sin_rot, ch_tot)
-    local = lax.all_to_all(spectrum, "chan", split_axis=1, concat_axis=0, tiled=True)
+    pieces = jnp.split(spectrum, lax.axis_size("chan"), axis=1)
+    received = lax.all_to_all(jnp.stack(pieces), "chan", 0, 0)
+    local = jnp.concatenate(received, axis=0)
     group_in = local.shape[0]
     own = local.reshape(group_in, CH_WIN, 2 * frames)
     keep_slots = n_stn // 2 + 1

time: 167 us -> 135 us (0.81)
  local copies, waits for them, and re-layouts: 41.5 us -> 9.1 us
    unnamed x6 -> x4, local copies, waits for them, and re-layouts: 19.2 us -> 1.37 us
    all_to_all x2 -> x0, local copies, waits for them, and re-layouts: 9.8 us -> none  [per_device(): lax.all_to_all(spectrum, 'chan', split_axis=1, concat_axis=0, tiled=True)]
    reshape x1, local copies, waits for them, and re-layouts: 4.94 us -> 0.02 us  [channelise(): return spectrum.reshape(count, ch_tot, 2, frames)]
    another operation x2 -> x3, other arithmetic: 4.58 us -> 5.32 us
  transfers between devices with their start and end apart: 4 -> 4, of which waited for: 3 -> 3; matrix products, arithmetic and copies ran while one was open for 2% -> 3% of each run, Pallas kernels for 0% -> 0%
where the time goes in v1:
time: 135 us
  other arithmetic  87.5 us (65%)
  matrix products  17.5 us (13%)
  waiting for transfers between devices  11.6 us (9%)
  starting transfers between devices  9.16 us (7%)
  local copies, waits for them, and re-layouts  9.1 us (7%)
    convert_element_type x1, other arithmetic, twiddles(): sines = jnp.sin(phase).astype(jnp.bfloat16)  35.1 us
    neg x1, other arithmetic, twiddles(): upper = jnp.concatenate([cosines, -sines], axis=1)  32.3 us
    dot_general x1, matrix products, channelise(): jnp.dot(lhs, table, preferred_element_type=jnp.float32)  13.7 us
    ppermute x3, waiting for transfers between devices, from_behind(): lax.ppermute(value, axis, [(i, (i + by) % devices) for i in range(devices)])  9.23 us
    ppermute x3, starting transfers between devices, from_behind(): lax.ppermute(value, axis, [(i, (i + by) % devices) for i in range(devices)])  4.9 us
    another operation x1, other arithmetic, channelise(): lhs = jnp.stack([rot_real, rot_imag], axis=3).astype(jnp.bfloat16)  4.84 us
    another operation x2, other arithmetic  4.58 us
    all_to_all x1, starting transfers between devices, per_device(): received = lax.all_to_all(jnp.stack(pieces), 'chan', 0, 0)  4.26 us
  transfers between devices with their start and end apart: 4, of which 3 were waited for; matrix products, arithmetic and copies ran while one was open for 3% of the time, Pallas kernels for 0%

profile of v1, /device:TPU:0, one launch (start us, length us, event | category | flops | bytes accessed | tf_op | source)
XLA Modules:
  0.0 135.0 jit_solution(623482681187098051)
XLA Ops:
  0.0 2.4 %fusion.29 = f32[131072]{0:T(1024)S(1)} fusion(), kind=kLoop, calls=%fused_computation.45 | loop fusion | flops 5373952 | bytes 524288 | tf_op jit(solution)/shard_map/mul | solution.py:22
  2.4 2.1 %fusion.41 = (f32[16,8192]{1,0:T(8,128)S(1)}, f32[16,8192]{1,0:T(8,128)S(1)}) fusion(), kind=kLoop, calls=%fused_computation.65 | loop fusion | flops 1966080 | bytes 1048576 | tf_op jit(solution)/shard_map/sin | solution.py:41
  4.5 35.1 %sine_convert_fusion = (bf16[8192,256]{1,0:T(8,128)(2,1)}, bf16[8192,256]{1,0:T(8,128)(2,1)}) fusion(), kind=kLoop, calls=%fused_computation.15 | loop fusion | flops 33554432 | bytes 8388608 | tf_op jit(solution)/shard_map/convert_element_type | solution.py:30
  39.5 32.3 %fusion.14 = bf16[8192,256]{1,0:T(8,128)(2,1)} fusion(), kind=kLoop, calls=%fused_computation.24 | loop fusion | flops 37748736 | bytes 4194304 | tf_op jit(solution)/shard_map/neg | solution.py:31
  71.9 2.1 %multiply_add_fusion.1 = f32[2,2,2,8192]{3,2,1,0:T(2,128)S(1)} fusion(bf16[2,17,2,8192]{3,2,1,0:T(2,128)(2,1)S(1)} %copy-done, f32[8192]{0:T(1024)S(1)} %get-tuple-element.19, f32[8192]{0:T(1024)S(1)} %get-tuple-element.20, f32[8192]{0:T(1024)S(1)} %get-tuple-element.21, f32[8192]{0:T(1024)S(1)} %get-tuple-element.22, f32[8192]{0:T(1024)S(1)} %get-tuple-element.23, ...), kind=kLoop, calls=%fused_computation.67 | loop fusion | flops 3080192 | bytes 2883584 | tf_op jit(solution)/shard_map/add | solution.py:51
  74.0 0.2 fusion.53
  74.2 0.2 copy_bitcast_fusion.1
  74.4 4.4 %add_convert_fusion = (bf16[16,2,2,1,8192]{4,3,2,1,0:T(2,128)(2,1)S(1)}, bf16[16,2,2,1,8192]{4,3,2,1,0:T(2,128)(2,1)S(1)}) fusion(f32[16,8192]{1,0:T(8,128)S(1)} %get-tuple-element.44, f32[2,2,8192]{2,1,0:T(2,128)S(1)} %get-tuple-element.42, f32[16,8192]{1,0:T(8,128)S(1)} %get-tuple-element.45, f32[2,2,8192]{2,1,0:T(2,128)S(1)} %get-tuple-element.43), kind=kLoop, calls=%fused_computation.23 | loop fusion | flops 4194304 | bytes 3407872 | tf_op jit(solution)/shard_map/convert
  78.8 4.8 %pad_maximum_fusion = bf16[16,2,2,2,8192]{4,3,2,1,0:T(2,128)(2,1)S(1)} fusion(bf16[16,2,2,1,8192]{4,3,2,1,0:T(2,128)(2,1)S(1)} %get-tuple-element.17, bf16[16,2,2,1,8192]{4,3,2,1,0:T(2,128)(2,1)S(1)} %get-tuple-element.16), kind=kLoop, calls=%fused_computation.21 | loop fusion | flops 4194304 | bytes 4194304 | tf_op jit(solution)/shard_map/stack | solution.py:58
  83.7 1.2 copy.55
  84.9 13.7 %fusion.19 = bf16[64,512]{1,0:T(8,128)(2,1)S(1)} fusion(bf16[64,16384]{1,0:T(8,128)(2,1)S(1)} %bitcast.55, bf16[8192,256]{1,0:T(8,128)(2,1)} %get-tuple-element.47, bf16[8192,256]{1,0:T(8,128)(2,1)} %get-tuple-element.46, bf16[8192,256]{1,0:T(8,128)(2,1)} %fusion.14), kind=kOutput, calls=%fused_computation.28 | convolution fusion | flops 1140916224 | bytes 14745600 | tf_op jit(solution)/shard_map/dot_general | solution.py:60
  98.7 0.7 pad_maximum_fusion.4
  99.5 4.3 %all-to-all-start = ((bf16[4,2,1024,2,2]{2,4,3,1,0:T(2,128)(2,1)}), bf16[4,2,1024,2,2]{2,4,3,1,0:T(2,128)(2,1)S(1)}, u32[]{:S(2)}, u32[]{:S(2)}) async-start(bf16[4,2,1024,2,2]{2,4,3,1,0:T(2,128)(2,1)} %pad_maximum_fusion.4), calls=%async_computation | async-start | bytes 131072 | tf_op jit(solution)/shard_map/all_to_all | solution.py:96
  103.7 0.7 fusion.51
  104.4 0.7 compare_bitcast_fusion
  105.1 0.2 reduce-window.7
  105.3 0.2 select_reduce_fusion
  105.5 2.3 %all-to-all-done = bf16[4,2,1024,2,2]{2,4,3,1,0:T(2,128)(2,1)S(1)} async-done(((bf16[4,2,1024,2,2]{2,4,3,1,0:T(2,128)(2,1)}), bf16[4,2,1024,2,2]{2,4,3,1,0:T(2,128)(2,1)S(1)}, u32[]{:S(2)}, u32[]{:S(2)}) %all-to-all-start) | async-done | bytes 65568 | tf_op jit(solution)/shard_map/all_to_all | solution.py:96
  107.9 2.2 %collective-permute-start = (bf16[1,8,1024,4]{2,1,3,0:T(8,128)(2,1)S(1)}, bf16[1,8,1024,4]{2,1,3,0:T(8,128)(2,1)S(1)}, u32[]{:S(2)}, u32[]{:S(2)}) collective-permute-start(bf16[1,8,1024,4]{2,1,3,0:T(8,128)(2,1)S(1)} %copy.51), channel_id=1, source_target_pairs={{0,4},{4,8},{8,12},{12,16},{16,20},{20,24},{24,28},{28,0},{1,5},{5... | collective-permute-start | bytes 196616 | tf_op jit(solution)/shard_map/ppermute | solution.py:15
  110.2 5.3 %collective-permute-done = bf16[1,8,1024,4]{2,1,3,0:T(8,128)(2,1)S(1)} collective-permute-done((bf16[1,8,1024,4]{2,1,3,0:T(8,128)(2,1)S(1)}, bf16[1,8,1024,4]{2,1,3,0:T(8,128)(2,1)S(1)}, u32[]{:S(2)}, u32[]{:S(2)}) %collective-permute-start) | collective-permute-done | bytes 65568 | tf_op jit(solution)/shard_map/ppermute | solution.py:15
  115.5 0.2 fusion.43
  115.8 0.1 broadcast_in_dim.76
  116.1 2.6 %collective-permute-start.2 = (bf16[8,1024,4]{1,0,2:T(8,128)(2,1)S(1)}, bf16[8,1024,4]{1,0,2:T(8,128)(2,1)S(1)}, u32[]{:S(2)}, u32[]{:S(2)}) collective-permute-start(bf16[8,1024,4]{1,0,2:T(8,128)(2,1)S(1)} %copy.49), channel_id=1, source_target_pairs={{0,16},{4,20},{8,24},{12,28},{16,0},{20,4},{24,8},{28,12},{1,17},{... | collective-permute-start | bytes 196616 | tf_op jit(solution)/shard_map/ppermute | solution.py:15
  118.7 1.4 %copy.45 = bf16[8,1024,4]{0,2,1:T(4,128)(2,1)} copy(bf16[8,1024,4]{1,2,0:T(4,128)(2,1)S(1)} %reshape.388) | data formatting | bytes 131072 | tf_op jit(solution)/shard_map/reshape;reshape | solution.py:99
  120.1 4.0 %collective-permute-done.2 = bf16[8,1024,4]{1,0,2:T(8,128)(2,1)S(1)} collective-permute-done((bf16[8,1024,4]{1,0,2:T(8,128)(2,1)S(1)}, bf16[8,1024,4]{1,0,2:T(8,128)(2,1)S(1)}, u32[]{:S(2)}, u32[]{:S(2)}) %collective-permute-start.2) | collective-permute-done | bytes 65568 | tf_op jit(solution)/shard_map/ppermute | solution.py:15
  124.1 1.4 %copy.43 = bf16[40,1024,4]{0,2,1:T(4,128)(2,1)} copy(bf16[40,1024,4]{1,0,2:T(8,128)(2,1)S(1)} %copy_bitcast_fusion) | data formatting | bytes 655360 | tf_op jit(solution)/shard_map/reshape | solution.py:116
  125.5 1.4 %copy.44 = bf16[40,1024,4]{0,2,1:T(4,128)(2,1)} copy(bf16[40,1024,4]{1,0,2:T(8,128)(2,1)S(1)} %pad_maximum_fusion.2) | data formatting | bytes 655360 | tf_op jit(solution)/shard_map/concatenate | solution.py:68
  127.0 3.8 %multiply_convert_fusion = bf16[1024,8,80]{2,1,0:T(8,128)(2,1)S(1)} fusion(bf16[8,1024,4]{0,2,1:T(4,128)(2,1)} %copy.45, bf16[40,1024,4]{0,2,1:T(4,128)(2,1)} %copy.44, bf16[40,1024,4]{0,2,1:T(4,128)(2,1)} %copy.43), kind=kOutput, calls=%fused_computation.20 | convolution fusion | flops 7864320 | bytes 2031616 | tf_op jit(solution)/shard_map/dot_general | solution.py:70
  130.7 2.0 %copy.46 = bf16[1024,8,80]{0,2,1:T(8,128)(2,1)S(1)} copy(bf16[1024,8,80]{2,1,0:T(8,128)(2,1)S(1)} %multiply_convert_fusion) | data formatting | bytes 2621440 | tf_op jit(solution)/shard_map/convert_element_type | solution.py:117
  132.7 0.1 copy.47
  132.9 0.6 gather_fusion
  133.5 1.5 %fusion.15 = bf16[8,2,1024,40]{2,3,1,0:T(8,128)(2,1)} fusion(pred[40]{0:T(512)(128)(4,1)S(1)} %broadcast_in_dim.76, pred[40]{0:T(512)(128)(4,1)S(1)} %broadcast_in_dim.71, bf16[5,8,2,1024,8]{3,4,2,1,0:T(8,128)(2,1)S(1)} %gather_fusion), kind=kLoop, calls=%fused_computation.26 | loop fusion | flops 1310720 | bytes 2621520 | tf_op jit(solution)/shard_map/jit(_where)/select_n | solution.py:121
  (24 shorter events, 0.7 us)
Async XLA Ops:
  39.5 32.4 %copy-start = (bf16[2,17,2,8192]{3,2,1,0:T(2,128)(2,1)S(1)}, bf16[2,17,2,8192]{3,2,1,0:T(2,128)(2,1)}, u32[]{:S(2)}) copy-start(bf16[2,17,2,8192]{3,2,1,0:T(2,128)(2,1)} %param.2) | copy-start | bytes 3342340
  99.5 8.4 %all-to-all-start = ((bf16[4,2,1024,2,2]{2,4,3,1,0:T(2,128)(2,1)}), bf16[4,2,1024,2,2]{2,4,3,1,0:T(2,128)(2,1)S(1)}, u32[]{:S(2)}, u32[]{:S(2)}) async-start(bf16[4,2,1024,2,2]{2,4,3,1,0:T(2,128)(2,1)} %pad_maximum_fusion.4), calls=%async_computation | async-start | bytes 131072 | tf_op jit(solution)/shard_map/all_to_all | solution.py:96
  107.9 7.5 %collective-permute-start = (bf16[1,8,1024,4]{2,1,3,0:T(8,128)(2,1)S(1)}, bf16[1,8,1024,4]{2,1,3,0:T(8,128)(2,1)S(1)}, u32[]{:S(2)}, u32[]{:S(2)}) collective-permute-start(bf16[1,8,1024,4]{2,1,3,0:T(8,128)(2,1)S(1)} %copy.51), channel_id=1, source_target_pairs={{0,4},{4,8},{8,12},{12,16},{16,20},{20,24},{24,28},{28,0},{1,5},{5... | collective-permute-start | bytes 196616 | tf_op jit(solution)/shard_map/ppermute | solution.py:15
  115.4 8.6 %collective-permute-start.1 = (bf16[2,8,1024,4]{2,1,3,0:T(8,128)(2,1)S(1)}, bf16[2,8,1024,4]{2,1,3,0:T(8,128)(2,1)S(1)}, u32[]{:S(2)}, u32[]{:S(2)}) collective-permute-start(bf16[2,8,1024,4]{2,1,3,0:T(8,128)(2,1)S(1)} %pad_maximum_fusion.3), channel_id=1, source_target_pairs={{0,8},{4,12},{8,16},{12,20},{16,24},{20,28},{24,0},{28,4},{1,9},{5... | collective-permute-start | bytes 393224 | tf_op jit(solution)/shard_map/ppermute | solution.py:15
  116.1 8.0 %collective-permute-start.2 = (bf16[8,1024,4]{1,0,2:T(8,128)(2,1)S(1)}, bf16[8,1024,4]{1,0,2:T(8,128)(2,1)S(1)}, u32[]{:S(2)}, u32[]{:S(2)}) collective-permute-start(bf16[8,1024,4]{1,0,2:T(8,128)(2,1)S(1)} %copy.49), channel_id=1, source_target_pairs={{0,16},{4,20},{8,24},{12,28},{16,0},{20,4},{24,8},{28,12},{1,17},{... | collective-permute-start | bytes 196616 | tf_op jit(solution)/shard_map/ppermute | solution.py:15
